TPU v7x, 32 devices: a whole 2x2x4 slice. The times are simulated.
32 devices in a mesh: replica: 4 (over y, core), table: 8 (over z, x).
Axes of the slice: x: 2, y: 2, z: 4, core: 2. Of those that a mesh axis runs over, the one named last changes fastest.
Arguments:
- cache: float32 [768, 16384], P('table', 'replica'), may hold values from -6 to 6
- accum: float32 [768, 16384], P('table', 'replica'), may hold values from 0.5 to 8
- row_ids: int32 [4, 8, 128], P('replica'), may hold values from 0 to 4095
- lengths: int32 [4, 8], P('replica'), may hold values from 1 to 128, 614 in all within a row
- seq_slot: int32 [4, 8], P('replica'), may hold values from 0 to 7, each once within a row
- block_mask: int32 [4, 8, 2, 2], P('replica'), may hold values 0 or 1
- cotangent: bfloat16 [4, 1024, 768], P('replica', 'table'), may hold values from -6 to 6
- w_uqkv: bfloat16 [768, 3072], P('replica'), may hold values from -0.21875 to 0.21875
- w_out: bfloat16 [768, 768], P('replica'), may hold values from -0.21875 to 0.21875
- w2_accum: float32 [768, 768], P('replica', 'table'), may hold values from 81.92 to 8192
Outputs:
- cache_new: float32 [768, 16384], P('table', 'replica')
- accum_new: float32 [768, 16384], P('table', 'replica')
- w2_step: float32 [768, 768], P('replica', 'table')
Inputs may be any that keep to these rules, and one draw needn't show every extreme that they name: `lengths`: in every replica group some sequence has length 128. `seq_slot`: each row names every slot once.
All inputs are finite; a program needn't handle non-finite values. No bound on the sum of `block_mask` on one device may be relied on, other than what follows from the above.
Results may differ from a plain program's by a relative error of at most 0.012.
Values may be sent and summed in bfloat16 or wider, within the bound.
A program may use at most 64 MiB of HBM per device.

v0:
```python
from functools import partial
import jax
import jax.numpy as jnp
from jax import lax
from jax.sharding import PartitionSpec as P

D = 768
HEADS = 12
HEAD_DIM = 64
SEQ_DEV = 1
SEQ_LEN = 128
CAP = 128
EPS_NORM = 1e-05
EPS_ATTN = 1e-06
STEP_SIZE = 0.5


def normalize(row_data):
    centred = row_data - jnp.mean(row_data, axis=-1, keepdims=True)
    variance = jnp.mean(centred * centred, axis=-1, keepdims=True)
    return centred / jnp.sqrt(variance + EPS_NORM)


def pattern_mask(lengths_at, blocks_at, seq_len):
    block_count = blocks_at.shape[-1]
    block_width = seq_len // block_count
    places = jnp.arange(seq_len, dtype=jnp.int32)
    block_of = places // block_width
    same_block = block_of[:, None] == block_of[None, :]
    chosen = jnp.repeat(jnp.repeat(blocks_at, block_width, axis=1), block_width, axis=2) > 0
    chosen = chosen | same_block[None]
    causal = places[None, :] <= places[:, None]
    inside = places[None, :] < lengths_at[:, None]
    allowed = chosen & causal[None] & inside[:, :, None] & inside[:, None, :]
    return (allowed.astype(jnp.float32), inside)


def attention_branch(hidden_pre, allowed):
    slot_count = allowed.shape[0]
    seq_len = allowed.shape[1]
    projected = jax.nn.silu(hidden_pre).astype(jnp.bfloat16)
    gate_u = projected[:, :D]
    queries = projected[:, D : 2 * D].reshape(slot_count, seq_len, HEADS, HEAD_DIM)
    key_rows = projected[:, 2 * D : 3 * D].reshape(slot_count, seq_len, HEADS, HEAD_DIM)
    value_rows = projected[:, 3 * D :].reshape(slot_count, seq_len, HEADS, HEAD_DIM)
    scores = jnp.einsum(
        "sihd,sjhd->shij", queries, key_rows, preferred_element_type=jnp.float32
    ) * HEAD_DIM ** (-0.5)
    weights = (jax.nn.silu(scores) * allowed[:, None]).astype(jnp.bfloat16)
    attended = jnp.einsum(
        "shij,sjhd->sihd", weights, value_rows, preferred_element_type=jnp.float32
    )
    attended = attended.reshape(slot_count * seq_len, D)
    centred_att = attended - jnp.mean(attended, axis=-1, keepdims=True)
    inverse_dev = 1.0 / jnp.sqrt(
        jnp.mean(centred_att * centred_att, axis=-1, keepdims=True) + EPS_ATTN
    )
    return centred_att * inverse_dev * gate_u.astype(jnp.float32)


def body(cache, accum, row_ids, lengths, seq_slot, block_mask, cotangent, w_uqkv, w_out, w2_accum):
    tables = lax.axis_size("table")
    table_index = lax.axis_index("table")
    columns = cache.shape[0]
    seq_count = seq_slot.shape[1]
    sequence_ids = jnp.arange(seq_count, dtype=jnp.int32)
    matches = (seq_slot[0][:, None] == sequence_ids[None, :]).astype(jnp.int32)
    seq_at = jnp.sum(sequence_ids[:, None] * matches, axis=0)
    lengths_at = jnp.sum(lengths[0][:, None] * matches, axis=0)
    slot_ids = row_ids[0][seq_at].reshape(-1)
    own_first = table_index * SEQ_DEV
    own_lengths = lax.dynamic_slice_in_dim(lengths_at, own_first, SEQ_DEV, 0)
    own_blocks = lax.dynamic_slice_in_dim(block_mask[0][seq_at], own_first, SEQ_DEV, 0)
    allowed, inside = pattern_mask(own_lengths, own_blocks, SEQ_LEN)
    picked = jnp.take(cache, slot_ids, axis=1).astype(jnp.bfloat16).reshape(columns, tables, CAP)
    arrived = lax.all_to_all(picked, "table", split_axis=1, concat_axis=0, tiled=True)
    embedded = arrived.reshape(D, CAP).T
    row_float = embedded.astype(jnp.float32)
    normed = normalize(row_float).astype(jnp.bfloat16)
    full_uqkv = lax.all_gather(w_uqkv, "replica", axis=0, tiled=True)
    hidden_pre = jnp.dot(normed, full_uqkv, preferred_element_type=jnp.float32)
    live_cot = cotangent[0] * inside.reshape(-1)[:, None].astype(jnp.bfloat16)
    d_gated = lax.dot_general(
        live_cot,
        lax.all_gather(w_out, "replica", axis=0, tiled=True),
        (((1,), (1,)), ((), ())),
        preferred_element_type=jnp.float32,
    )
    gated_raw, branch_vjp = jax.vjp(partial(attention_branch, allowed=allowed), hidden_pre)
    gated = gated_raw.astype(jnp.bfloat16)
    d_hidden = branch_vjp(d_gated)[0].astype(jnp.bfloat16)
    d_normed = lax.dot_general(
        d_hidden, full_uqkv, (((1,), (1,)), ((), ())), preferred_element_type=jnp.float32
    )
    _, norm_vjp = jax.vjp(normalize, row_float)
    row_grad = live_cot.astype(jnp.float32) + norm_vjp(d_normed)[0]
    sending = row_grad.T.reshape(tables, columns, CAP)
    returned = lax.all_to_all(sending, "table", split_axis=0, concat_axis=2, tiled=True).reshape(
        columns, tables * CAP
    )
    grad_cols = jnp.zeros_like(cache).at[:, slot_ids].add(returned)
    accum_next = accum + grad_cols * grad_cols
    cache_next = cache - STEP_SIZE * grad_cols / jnp.sqrt(accum_next)
    full_grad = lax.dot_general(
        gated, live_cot, (((0,), (0,)), ((), ())), preferred_element_type=jnp.float32
    )
    by_columns = lax.psum_scatter(full_grad, "table", scatter_dimension=1, tiled=True)
    summed = lax.psum_scatter(by_columns, "replica", scatter_dimension=0, tiled=True)
    w2_step = summed / jnp.sqrt(w2_accum + summed * summed)
    return (cache_next, accum_next, w2_step)


def solution(mesh):
    return jax.shard_map(
        body,
        mesh=mesh,
        in_specs=(
            P("table", "replica"),
            P("table", "replica"),
            P("replica", None, None),
            P("replica", None),
            P("replica", None),
            P("replica", None, None, None),
            P("replica", "table", None),
            P("replica", None),
            P("replica", None),
            P("replica", "table"),
        ),
        out_specs=(P("table", "replica"), P("table", "replica"), P("replica", "table")),
        check_vma=False,
    )
```

profile of v0, /device:TPU:0, one launch (start us, length us, event | category | flops | bytes accessed | tf_op | source)
XLA Modules:
  0.0 180.1 jit_solution(12258738646778073409)
XLA Ops:
  7.9 1.8 %copy.119 = f32[96,4096]{0,1:T(8,128)S(1)} copy(f32[96,4096]{1,0:T(8,128)} %param.10) | data formatting | bytes 3145728 | tf_op args[0]
  10.5 2.9 %gather_fusion.1 = bf16[1024,96]{1,0:T(8,128)(2,1)S(1)} fusion(f32[96,4096]{0,1:T(8,128)S(1)} %copy.119, s32[1024]{0:T(1024)S(1)} %broadcast_clamp_fusion), kind=kCustom, calls=%fused_computation.1 | custom fusion | bytes 397312 | tf_op jit(solution)/shard_map/jit(_take)/gather | solution.py:75
  14.3 7.3 %all-to-all-start = ((bf16[96,8,128]{2,0,1:T(8,128)(2,1)}), bf16[96,8,128]{2,0,1:T(8,128)(2,1)S(1)}, u32[]{:S(2)}, u32[]{:S(2)}) async-start(bf16[96,8,128]{2,0,1:T(8,128)(2,1)} %select_convert_fusion), calls=%async_computation | async-start | bytes 393216 | tf_op jit(solution)/shard_map/all_to_all | solution.py:76
  25.5 4.1 %all-to-all-done = bf16[96,8,128]{2,0,1:T(8,128)(2,1)S(1)} async-done(((bf16[96,8,128]{2,0,1:T(8,128)(2,1)}), bf16[96,8,128]{2,0,1:T(8,128)(2,1)S(1)}, u32[]{:S(2)}, u32[]{:S(2)}) %all-to-all-start) | async-done | bytes 196640 | tf_op jit(solution)/shard_map/all_to_all | solution.py:76
  30.6 19.1 %all-gather.5.cloned.1.call-done = bf16[768,3072]{1,0:T(8,128)(2,1)} async-done(((bf16[192,3072]{1,0:T(8,128)(2,1)}), bf16[768,3072]{1,0:T(8,128)(2,1)}) %all-gather.5.cloned.1.call-update) | async-done | bytes 4718608 | tf_op jit(solution)/shard_map/all_gather | solution.py:80
  49.7 4.4 %multiply_convert_fusion = (bf16[128,3072]{1,0:T(8,128)(2,1)S(1)}, f32[128,3072]{1,0:T(8,128)}) fusion(bf16[768,3072]{1,0:T(8,128)(2,1)} %all-gather.5.cloned.1.call-done, f32[768,128]{0,1:T(8,128)S(1)} %copy.103, f32[128]{0:T(128)S(1)} %get-tuple-element.31, f32[128]{0:T(128)S(1)} %broadcast_multiply_fusion.1), kind=kOutput, calls=%fused_computation.12 | convolution fusion | flops 606240768 | bytes 7472128 | tf_op jit(solution)/shard_map/dot_general | solution.py:81
  60.1 8.7 %all-gather.3.cloned.1.call-done = bf16[768,768]{1,0:T(8,128)(2,1)} async-done(((bf16[192,768]{1,0:T(8,128)(2,1)}), bf16[768,768]{1,0:T(8,128)(2,1)}) %all-gather.3.cloned.1.call-update) | async-done | bytes 1179664 | tf_op jit(solution)/shard_map/all_gather | solution.py:85
  68.8 1.9 %multiply_reduce_fusion = (f32[128]{0:T(128)S(1)}, f32[128,768]{1,0:T(8,128)S(1)}) fusion(f32[128,768]{1,0:T(8,128)S(1)} %copy.110, f32[128]{0:T(128)S(1)} %broadcast_multiply_fusion, bf16[128,3072]{1,0:T(8,128)(2,1)} %copy-done.2, bf16[768,768]{1,0:T(8,128)(2,1)} %all-gather.3.cloned.1.call-done, bf16[1,128,768]{2,1,0:T(8,128)(2,1)S(1)} %copy-done.3, ...), kind=kOutput, calls=%fused_computation.56 | convolution fusion | flops 151584640 | bytes 2360576 | tf_op jit(solution)/shard_map/dot_general | solution.py:83
  71.8 3.0 %fusion.28 = f32[768,768]{0,1:T(8,128)} fusion(f32[128,768]{1,0:T(8,128)S(1)} %copy.110, f32[128]{0:T(128)S(1)} %broadcast_multiply_fusion, f32[128]{0:T(128)S(1)} %get-tuple-element.33, bf16[1,128,768]{2,1,0:T(8,128)(2,1)S(1)} %copy-done.3, bf16[128,3072]{1,0:T(8,128)(2,1)} %copy-done.2, bf16[128]{0:T(256)(128)(2,1)S(1)} %fusion.48), kind=kOutput, calls=%fused_computation.59 | convolution fusion | flops 151584768 | bytes 3147008 | tf_op jit(solution)/shard_map/dot_general | solution.py:104
  74.8 1.8 %fusion.50 = (f32[128]{0:T(128)S(1)}, f32[128,768]{1,0:T(8,128)S(1)}, bf16[128,768]{1,0:T(8,128)(2,1)}) fusion(f32[128]{0:T(128)} %get-tuple-element.32, f32[128,768]{1,0:T(8,128)S(1)} %copy.110, f32[128]{0:T(128)S(1)} %broadcast_multiply_fusion, f32[128]{0:T(128)} %copy-done.12, f32[128,768]{1,0:T(8,128)S(1)} %get-tuple-element.41, ...), kind=kLoop, calls=%fused_computation.111 | loop fusion | flops 1081216 | bytes 1574912 | tf_op jit(solution)/shard_map/transpose(jvp())/reduce_sum | solution.py:54
  77.6 1.8 fusion.11
  80.5 1.8 copy.114
  82.2 1.8 %fusion.55 = bf16[12,128,64]{1,2,0:T(8,128)(2,1)} fusion(bf16[12,128,128]{2,1,0:T(8,128)(2,1)S(1)} %fusion.11, bf16[128,12,64]{0,2,1:T(8,128)(2,1)} %bitcast.125), kind=kOutput, calls=%fused_computation.116 | convolution fusion | flops 25165824 | bytes 786432 | tf_op jit(solution)/shard_map/transpose(jvp(sihd,sjhd->shij))/dot_general | solution.py:46
  84.1 1.7 copy.113
  87.2 5.0 %fusion.25 = (f32[128]{0:T(128)S(1)}, f32[128,768]{1,0:T(8,128)S(1)}) fusion(f32[768,128]{0,1:T(8,128)S(1)} %copy.103, f32[128]{0:T(128)S(1)} %copy-done.23, f32[128]{0:T(128)S(1)} %copy-done.14, bf16[768,3072]{1,0:T(8,128)(2,1)} %all-gather.5.cloned.1.call-done, f32[128,3072]{1,0:T(8,128)} %get-tuple-element.35, bf16[128,768]{1,0:T(8,128)(2,1)} %get-tuple-element.26, ...), kind=kOutput, calls=%fused_computation.53 | convolution fusion | flops 611450752 | bytes 7865856 | tf_op jit(solution)/shard_map/dot_general | solution.py:92
  93.5 5.5 %all-to-all-start.1 = ((f32[8,96,128]{2,1,0:T(8,128)}), f32[8,96,128]{2,1,0:T(8,128)S(1)}, u32[]{:S(2)}, u32[]{:S(2)}) async-start(f32[8,96,128]{2,1,0:T(8,128)} %bitcast.40), calls=%async_computation.1 | async-start | bytes 786432 | tf_op jit(solution)/shard_map/all_to_all | solution.py:98
  99.1 2.8 %copy.118 = f32[96,4096]{0,1:T(8,128)} copy(f32[96,4096]{1,0:T(8,128)} %param.11) | data formatting | bytes 3145728 | tf_op args[1]
  102.0 13.1 %all-to-all-done.1 = f32[8,96,128]{2,1,0:T(8,128)S(1)} async-done(((f32[8,96,128]{2,1,0:T(8,128)}), f32[8,96,128]{2,1,0:T(8,128)S(1)}, u32[]{:S(2)}, u32[]{:S(2)}) %all-to-all-start.1) | async-done | bytes 393248 | tf_op jit(solution)/shard_map/all_to_all | solution.py:98
  115.6 7.4 %scatter_custom_fusion = f32[96,4096]{0,1:T(8,128)} fusion(s32[1024]{0:T(1024)S(1)} %bitcast.135, f32[1024,96]{1,0:T(8,128)S(1)} %copy.117, f32[]{:T(128)} %constant.61.clone.1), kind=kCustom, calls=%fused_computation.22 | custom fusion | flops 98304 | bytes 1572868 | tf_op jit(solution)/shard_map/scatter-add | solution.py:101
  123.0 26.4 %reduce-scatter.5.cloned.1.call-done = f32[768,96]{0,1:T(8,128)} async-done(((f32[768,768]{0,1:T(8,128)}), f32[768,96]{0,1:T(8,128)}) %reduce-scatter.5.cloned.1.call-update) | async-done | bytes 294928 | tf_op jit(solution)/shard_map/reduce_scatter | solution.py:107
  149.4 1.9 %copy.124 = f32[768,96]{1,0:T(8,128)} copy(f32[768,96]{0,1:T(8,128)} %reduce-scatter.5.cloned.1.call-done) | data formatting | bytes 589824
  151.3 4.6 %multiply_subtract_fusion = (f32[96,4096]{0,1:T(8,128)}, f32[96,4096]{0,1:T(8,128)}) fusion(f32[96,4096]{0,1:T(8,128)S(1)} %copy.119, f32[96,4096]{0,1:T(8,128)} %scatter_custom_fusion, f32[96,4096]{0,1:T(8,128)} %copy.118), kind=kLoop, calls=%fused_computation.5 | loop fusion | flops 1966080 | bytes 7864320 | tf_op jit(solution)/shard_map/sub | solution.py:103
  156.0 2.9 %copy.121 = f32[96,4096]{1,0:T(8,128)} copy(f32[96,4096]{0,1:T(8,128)} %get-tuple-element.20) | data formatting | bytes 3145728
  160.6 11.2 %reduce-scatter.7.cloned.1.call-done = f32[192,96]{1,0:T(8,128)} async-done(((f32[768,96]{1,0:T(8,128)}), f32[192,96]{1,0:T(8,128)}) %reduce-scatter.7.cloned.1.call-update) | async-done | bytes 73744
  (112 shorter events, 22.9 us)
Async XLA Ops:
  7.2 2.7 %copy-start = (s32[1,8,128]{2,1,0:T(8,128)S(1)}, s32[1,8,128]{2,1,0:T(8,128)}, u32[]{:S(2)}) copy-start(s32[1,8,128]{2,1,0:T(8,128)} %param.12) | copy-start | bytes 12292
  7.2 42.6 %all-gather.5.cloned.1.call-start = ((), (), s32[]{:S(2)}) async-start(), calls=%async_computation.5 | async-start | bytes 5898240 | tf_op jit(solution)/shard_map/all_gather | solution.py:80
  7.9 1.9 %copy-start.21 = (s32[1,8]{1,0:T(1,128)S(1)}, s32[1,8]{1,0:T(1,128)}, u32[]{:S(2)}) copy-start(s32[1,8]{1,0:T(1,128)} %param.13) | copy-start | bytes 100
  7.9 1.9 %copy-start.22 = (s32[1,8]{1,0:T(1,128)S(1)}, s32[1,8]{1,0:T(1,128)}, u32[]{:S(2)}) copy-start(s32[1,8]{1,0:T(1,128)} %param.14) | copy-start | bytes 100
  10.5 11.9 %copy-start.16 = (s32[1,8,2,2]{1,3,2,0:T(2,128)S(1)}, s32[1,8,2,2]{1,3,2,0:T(2,128)}, u32[]{:S(2)}) copy-start(s32[1,8,2,2]{1,3,2,0:T(2,128)} %param.15) | copy-start | bytes 388
  14.3 15.2 %all-to-all-start = ((bf16[96,8,128]{2,0,1:T(8,128)(2,1)}), bf16[96,8,128]{2,0,1:T(8,128)(2,1)S(1)}, u32[]{:S(2)}, u32[]{:S(2)}) async-start(bf16[96,8,128]{2,0,1:T(8,128)(2,1)} %select_convert_fusion), calls=%async_computation | async-start | bytes 393216 | tf_op jit(solution)/shard_map/all_to_all | solution.py:76
  21.6 47.2 %all-gather.3.cloned.1.call-start = ((), (), s32[]{:S(2)}) async-start(), calls=%async_computation.4 | async-start | bytes 1474560 | tf_op jit(solution)/shard_map/all_gather | solution.py:85
  22.3 127.1 %reduce-scatter.5.cloned.1.call-start = ((), (), s32[]{:S(2)}) async-start(), calls=%async_computation.6 | async-start | bytes 2654208 | tf_op jit(solution)/shard_map/reduce_scatter | solution.py:107
  29.9 24.2 %copy-start.13 = (f32[128]{0:T(128)}, f32[128]{0:T(128)S(1)}, u32[]{:S(2)}) copy-start(f32[128]{0:T(128)S(1)} %broadcast_multiply_fusion.1) | copy-start | bytes 1540
  30.1 24.0 %copy-start.19 = (f32[128]{0:T(128)}, f32[128]{0:T(128)S(1)}, u32[]{:S(2)}) copy-start(f32[128]{0:T(128)S(1)} %fusion.23) | copy-start | bytes 1540
  30.6 23.5 %copy-start.17 = (f32[128]{0:T(128)}, f32[128]{0:T(128)S(1)}, u32[]{:S(2)}) copy-start(f32[128]{0:T(128)S(1)} %get-tuple-element.31) | copy-start | bytes 1540
  56.0 1.5 copy-start.7
  57.6 11.2 %copy-start.3 = (bf16[1,128,768]{2,1,0:T(8,128)(2,1)S(1)}, bf16[1,128,768]{2,1,0:T(8,128)(2,1)}, u32[]{:S(2)}) copy-start(bf16[1,128,768]{2,1,0:T(8,128)(2,1)} %param.16) | copy-start | bytes 589828
  68.8 1.9 %copy-start.15 = (f32[128]{0:T(128)S(1)}, f32[128]{0:T(128)}, u32[]{:S(2)}) copy-start(f32[128]{0:T(128)} %fusion.22) | copy-start | bytes 1540
  77.6 1.8 %copy-start.9 = (bf16[128,768]{0,1:T(8,128)(2,1)S(1)}, bf16[128,768]{0,1:T(8,128)(2,1)}, u32[]{:S(2)}) copy-start(bf16[128,768]{0,1:T(8,128)(2,1)} %copy-done.8) | copy-start | bytes 589828
  79.4 6.4 %copy-start.5 = (bf16[12,128,128]{2,1,0:T(8,128)(2,1)S(1)}, bf16[12,128,128]{2,1,0:T(8,128)(2,1)}, u32[]{:S(2)}) copy-start(bf16[12,128,128]{2,1,0:T(8,128)(2,1)} %copy-done.4) | copy-start | bytes 1179652
  80.5 6.7 %copy-start.14 = (f32[128]{0:T(128)S(1)}, f32[128]{0:T(128)}, u32[]{:S(2)}) copy-start(f32[128]{0:T(128)} %copy-done.13) | copy-start | bytes 1540
  80.5 6.7 %copy-start.23 = (f32[128]{0:T(128)S(1)}, f32[128]{0:T(128)}, u32[]{:S(2)}) copy-start(f32[128]{0:T(128)} %get-tuple-element.30) | copy-start | bytes 1540
  87.2 5.0 %copy-start.20 = (f32[128]{0:T(128)S(1)}, f32[128]{0:T(128)}, u32[]{:S(2)}) copy-start(f32[128]{0:T(128)} %copy-done.19) | copy-start | bytes 1540
  87.2 5.0 %copy-start.18 = (f32[128]{0:T(128)S(1)}, f32[128]{0:T(128)}, u32[]{:S(2)}) copy-start(f32[128]{0:T(128)} %copy-done.17) | copy-start | bytes 1540
  93.5 21.6 %all-to-all-start.1 = ((f32[8,96,128]{2,1,0:T(8,128)}), f32[8,96,128]{2,1,0:T(8,128)S(1)}, u32[]{:S(2)}, u32[]{:S(2)}) async-start(f32[8,96,128]{2,1,0:T(8,128)} %bitcast.40), calls=%async_computation.1 | async-start | bytes 786432 | tf_op jit(solution)/shard_map/all_to_all | solution.py:98
  99.0 2.9 %copy-start.11 = (f32[192,96]{1,0:T(8,128)S(1)}, f32[192,96]{1,0:T(8,128)}, u32[]{:S(2)}) copy-start(f32[192,96]{1,0:T(8,128)} %param.19) | copy-start | bytes 221188
  99.0 72.8 %reduce-scatter.7.cloned.1.call-start = ((), (), s32[]{:S(2)}) async-start(), calls=%async_computation.7 | async-start | bytes 491520
  156.0 2.9 %copy-start.1 = (f32[96,4096]{0,1:T(8,128)S(1)}, f32[96,4096]{0,1:T(8,128)}, u32[]{:S(2)}) copy-start(f32[96,4096]{0,1:T(8,128)} %get-tuple-element.21) | copy-start | bytes 4718596
  (6 other events, 5.9 us)
Sparse Core Ops, SparseCore 0:
  9.5 40.1 all-gather.4
  51.3 17.4 all-gather.2
  74.9 74.4 reduce-scatter.4
  151.8 20.0 reduce-scatter.6
where the time goes:
time: 181 us; the launch traced here: 180 us
  waiting for transfers between devices  84 us (46%)
  local copies, waits for them, and re-layouts  27.2 us (15%)
  matrix products  22.4 us (12%)
  other arithmetic  19.4 us (11%)
  between operations  14.2 us (8%)
  starting transfers between devices  12.9 us (7%)
    reduce_scatter x1, waiting for transfers between devices, body(): lax.psum_scatter(full_grad, 'table', scatter_dimension=1, tiled=True)  26.4 us
    all_gather x1, waiting for transfers between devices, body(): full_uqkv = lax.all_gather(w_uqkv, 'replica', axis=0, tiled=True)  19.1 us
    unnamed x57, local copies, waits for them, and re-layouts  15.3 us
    all_to_all x1, waiting for transfers between devices, body(): lax.all_to_all(sending, 'table', split_axis=0, concat_axis=2, tiled=True)  13.1 us
    unnamed x5, waiting for transfers between devices  12.6 us
    all_gather x1, waiting for transfers between devices, body(): lax.all_gather(w_out, 'replica', axis=0, tiled=True)  8.68 us
    scatter-add x1, other arithmetic, body(): grad_cols = jnp.zeros_like(cache).at[:, slot_ids].add(returned)  7.41 us
    all_to_all x1, starting transfers between devices, body(): lax.all_to_all(picked, 'table', split_axis=1, concat_axis=0, tiled=True)  7.28 us
  transfers between devices with their start and end apart: 6, of which 6 were waited for; matrix products, arithmetic and copies ran while one was open for 32% of the time, Pallas kernels for 0%

commit v1 on v0

--- a/solution.py
+++ b/solution.py
@@ -77,7 +77,14 @@
     embedded = arrived.reshape(D, CAP).T
     row_float = embedded.astype(jnp.float32)
     normed = normalize(row_float).astype(jnp.bfloat16)
-    full_uqkv = lax.all_gather(w_uqkv, "replica", axis=0, tiled=True)
+    size = lax.axis_size("replica")
+    forward = [(i, (i + 1) % size) for i in range(size)]
+    parts = [w_uqkv]
+    for far in range(1, size):
+        parts = [lax.ppermute(parts[0], "replica", forward), *parts]
+    whole = jnp.concatenate(parts, axis=0)
+    turn = (lax.axis_index("replica") + 1) * parts[-1].shape[0]
+    full_uqkv = jnp.roll(whole, turn, axis=0)
     hidden_pre = jnp.dot(normed, full_uqkv, preferred_element_type=jnp.float32)
     live_cot = cotangent[0] * inside.reshape(-1)[:, None].astype(jnp.bfloat16)
     d_gated = lax.dot_general(

time: 181 us -> 189 us (1.044)
  local copies, waits for them, and re-layouts: 27.2 us -> 38.2 us
  waiting for transfers between devices: 84 us -> 78.6 us
  other arithmetic: 19.4 us -> 23.3 us
    ppermute x0 -> x3, waiting for transfers between devices: none -> 24.9 us  [body(): parts = [lax.ppermute(parts[0], 'replica', forward), *parts]]
    all_gather x1 -> x0, waiting for transfers between devices: 19.1 us -> none  [body(): full_uqkv = lax.all_gather(w_uqkv, 'replica', axis=0, tiled=True)]
    all_gather x1, waiting for transfers between devices: 8.68 us -> 0.01 us  [body(): lax.all_gather(w_out, 'replica', axis=0, tiled=True)]
    unnamed x57 -> x76, local copies, waits for them, and re-layouts: 15.3 us -> 21.9 us
    all_to_all x1, waiting for transfers between devices: 4.07 us -> 1.43 us  [body(): lax.all_to_all(picked, 'table', split_axis=1, concat_axis=0, tiled=True)]
    unnamed x5 -> x4, waiting for transfers between devices: 12.6 us -> 12.1 us
  transfers between devices with their start and end apart: 6 -> 8, of which waited for: 6 -> 6; matrix products, arithmetic and copies ran while one was open for 32% -> 38% of each run, Pallas kernels for 0% -> 0%
where the time goes in v1:
time: 189 us; the launch traced here: 188 us
  waiting for transfers between devices  78.6 us (42%)
  local copies, waits for them, and re-layouts  38.2 us (20%)
  other arithmetic  23.3 us (12%)
  matrix products  21.6 us (11%)
  between operations  14.3 us (8%)
  starting transfers between devices  12.1 us (6%)
    reduce_scatter x1, waiting for transfers between devices, body(): lax.psum_scatter(full_grad, 'table', scatter_dimension=1, tiled=True)  26.7 us
    ppermute x3, waiting for transfers between devices, body(): parts = [lax.ppermute(parts[0], 'replica', forward), *parts]  24.9 us
    unnamed x76, local copies, waits for them, and re-layouts  21.9 us
    all_to_all x1, waiting for transfers between devices, body(): lax.all_to_all(sending, 'table', split_axis=0, concat_axis=2, tiled=True)  13.4 us
    unnamed x4, waiting for transfers between devices  12.1 us
    scatter-add x1, other arithmetic, body(): grad_cols = jnp.zeros_like(cache).at[:, slot_ids].add(returned)  7.42 us
    all_to_all x1, starting transfers between devices, body(): lax.all_to_all(picked, 'table', split_axis=1, concat_axis=0, tiled=True)  6.58 us
    dot_general x1, matrix products, body(): lax.dot_general(d_hidden, full_uqkv, (((1,), (1,)), ((), ())), preferred_...  5.33 us
  transfers between devices with their start and end apart: 8, of which 6 were waited for; matrix products, arithmetic and copies ran while one was open for 38% of the time, Pallas kernels for 0%

profile of v1, /device:TPU:0, one launch (start us, length us, event | category | flops | bytes accessed | tf_op | source)
XLA Modules:
  0.0 188.1 jit_solution(15683685219604209176)
XLA Ops:
  7.7 16.0 %collective-permute-done = bf16[192,3072]{1,0:T(8,128)(2,1)S(1)} collective-permute-done((bf16[192,3072]{1,0:T(8,128)(2,1)}, bf16[192,3072]{1,0:T(8,128)(2,1)S(1)}, u32[]{:S(2)}, u32[]{:S(2)}) %collective-permute-start) | collective-permute-done | bytes 1179680 | tf_op jit(solution)/shard_map/ppermute | solution.py:84
  23.8 1.8 copy.119
  26.9 2.9 %gather_fusion.1 = bf16[1024,96]{1,0:T(8,128)(2,1)S(1)} fusion(f32[96,4096]{0,1:T(8,128)S(1)} %copy.119, s32[1024]{0:T(1024)S(1)} %broadcast_clamp_fusion), kind=kCustom, calls=%fused_computation.1 | custom fusion | bytes 397312 | tf_op jit(solution)/shard_map/jit(_take)/gather | solution.py:75
  30.6 8.9 %collective-permute-done.1 = bf16[192,3072]{1,0:T(8,128)(2,1)} collective-permute-done((bf16[192,3072]{1,0:T(8,128)(2,1)S(1)}, bf16[192,3072]{1,0:T(8,128)(2,1)}, u32[]{:S(2)}, u32[]{:S(2)}) %collective-permute-start.1) | collective-permute-done | bytes 1179680 | tf_op jit(solution)/shard_map/ppermute | solution.py:84
  41.2 6.6 %all-to-all-start = ((bf16[96,8,128]{2,0,1:T(8,128)(2,1)}), bf16[96,8,128]{2,0,1:T(8,128)(2,1)S(1)}, u32[]{:S(2)}, u32[]{:S(2)}) async-start(bf16[96,8,128]{2,0,1:T(8,128)(2,1)} %select_convert_fusion), calls=%async_computation | async-start | bytes 393216 | tf_op jit(solution)/shard_map/all_to_all | solution.py:76
  57.3 1.9 %copy.103 = f32[768,128]{0,1:T(8,128)} copy(f32[768,128]{1,0:T(8,128)} %bitcast.118) | data formatting | bytes 786432 | tf_op jit(solution)/shard_map/convert_element_type | solution.py:78
  67.8 3.4 %multiply_convert_fusion = (bf16[128,3072]{1,0:T(8,128)(2,1)S(1)}, f32[128,3072]{1,0:T(8,128)}) fusion(bf16[1536,3072]{1,0:T(8,128)(2,1)S(1)} %constant_dynamic-update-slice_fusion, s32[]{:T(128)S(6)} %select_n.70, f32[768,128]{0,1:T(8,128)S(1)} %copy-done.3, f32[128]{0:T(128)S(1)} %get-tuple-element.31, f32[128]{0:T(128)S(1)} %broadcast_multiply_fusion.1), kind=kOutput, calls=%fused_computation.16 | convolution fusion | flops 606240768 | bytes 7472132 | tf_op jit(solution)/shard_map/dot_general | solution.py:88
  76.4 2.7 %multiply_reduce_fusion = (f32[128]{0:T(128)S(1)}, f32[128,768]{1,0:T(8,128)}) fusion(f32[128,768]{1,0:T(8,128)S(1)} %copy.110, f32[128]{0:T(128)S(1)} %broadcast_multiply_fusion, bf16[128,3072]{1,0:T(8,128)(2,1)} %copy-done.5, bf16[768,768]{1,0:T(8,128)(2,1)} %all-gather.2.cloned.1.call-done, bf16[1,128,768]{2,1,0:T(8,128)(2,1)S(1)} %copy-done.7, ...), kind=kOutput, calls=%fused_computation.59 | convolution fusion | flops 151584640 | bytes 2360576 | tf_op jit(solution)/shard_map/dot_general | solution.py:90
  80.2 2.0 %fusion.30 = f32[768,768]{0,1:T(8,128)} fusion(f32[128,768]{1,0:T(8,128)S(1)} %copy.110, f32[128]{0:T(128)S(1)} %broadcast_multiply_fusion, f32[128]{0:T(128)S(1)} %get-tuple-element.33, bf16[1,128,768]{2,1,0:T(8,128)(2,1)S(1)} %copy-done.7, bf16[128,3072]{1,0:T(8,128)(2,1)S(1)} %copy-done.6, bf16[128]{0:T(256)(128)(2,1)S(1)} %fusion.52), kind=kOutput, calls=%fused_computation.61 | convolution fusion | flops 151584768 | bytes 3147264 | tf_op jit(solution)/shard_map/dot_general | solution.py:111
  82.2 1.9 %fusion.54 = (f32[128]{0:T(128)S(1)}, f32[128,768]{1,0:T(8,128)S(1)}, bf16[128,768]{1,0:T(8,128)(2,1)}) fusion(f32[128]{0:T(128)} %get-tuple-element.32, f32[128,768]{1,0:T(8,128)S(1)} %copy.110, f32[128]{0:T(128)S(1)} %broadcast_multiply_fusion, f32[128]{0:T(128)} %copy-done.19, f32[128,768]{1,0:T(8,128)} %get-tuple-element.41, ...), kind=kLoop, calls=%fused_computation.123 | loop fusion | flops 1081216 | bytes 1574912 | tf_op jit(solution)/shard_map/transpose(jvp())/reduce_sum | solution.py:54
  85.1 1.8 fusion.14
  88.0 1.7 copy.114
  89.7 1.8 fusion.59
  91.6 1.8 copy.113
  94.7 5.3 %fusion.28 = (f32[128]{0:T(128)S(1)}, f32[128,768]{1,0:T(8,128)S(1)}) fusion(f32[768,128]{0,1:T(8,128)S(1)} %copy-done.4, f32[128]{0:T(128)S(1)} %copy-done.29, f32[128]{0:T(128)S(1)} %copy-done.21, bf16[1536,3072]{1,0:T(8,128)(2,1)} %copy-done.15, s32[]{:T(128)S(6)} %select_n.70, f32[128,3072]{1,0:T(8,128)} %get-tuple-element.35, ...), kind=kOutput, calls=%fused_computation.56 | convolution fusion | flops 611450752 | bytes 7865860 | tf_op jit(solution)/shard_map/dot_general | solution.py:99
  101.4 4.7 %all-to-all-start.1 = ((f32[8,96,128]{2,1,0:T(8,128)}), f32[8,96,128]{2,1,0:T(8,128)S(1)}, u32[]{:S(2)}, u32[]{:S(2)}) async-start(f32[8,96,128]{2,1,0:T(8,128)} %bitcast.40), calls=%async_computation.1 | async-start | bytes 786432 | tf_op jit(solution)/shard_map/all_to_all | solution.py:105
  106.2 2.8 %copy.118 = f32[96,4096]{0,1:T(8,128)} copy(f32[96,4096]{1,0:T(8,128)} %param.11) | data formatting | bytes 3145728 | tf_op args[1]
  109.2 13.4 %all-to-all-done.1 = f32[8,96,128]{2,1,0:T(8,128)S(1)} async-done(((f32[8,96,128]{2,1,0:T(8,128)}), f32[8,96,128]{2,1,0:T(8,128)S(1)}, u32[]{:S(2)}, u32[]{:S(2)}) %all-to-all-start.1) | async-done | bytes 393248 | tf_op jit(solution)/shard_map/all_to_all | solution.py:105
  123.1 7.4 %scatter_custom_fusion = f32[96,4096]{0,1:T(8,128)} fusion(s32[1024]{0:T(1024)S(1)} %bitcast.133, f32[1024,96]{1,0:T(8,128)S(1)} %copy.117, f32[]{:T(128)} %constant.82.clone.1), kind=kCustom, calls=%fused_computation.26 | custom fusion | flops 98304 | bytes 1572868 | tf_op jit(solution)/shard_map/scatter-add | solution.py:108
  130.5 26.7 %reduce-scatter.5.cloned.1.call-done = f32[768,96]{0,1:T(8,128)} async-done(((f32[768,768]{0,1:T(8,128)}), f32[768,96]{0,1:T(8,128)}) %reduce-scatter.5.cloned.1.call-update) | async-done | bytes 294928 | tf_op jit(solution)/shard_map/reduce_scatter | solution.py:114
  157.2 1.9 %copy.124 = f32[768,96]{1,0:T(8,128)} copy(f32[768,96]{0,1:T(8,128)} %reduce-scatter.5.cloned.1.call-done) | data formatting | bytes 589824
  159.1 4.6 %multiply_subtract_fusion = (f32[96,4096]{0,1:T(8,128)}, f32[96,4096]{0,1:T(8,128)}) fusion(f32[96,4096]{0,1:T(8,128)S(1)} %copy.119, f32[96,4096]{0,1:T(8,128)} %scatter_custom_fusion, f32[96,4096]{0,1:T(8,128)} %copy.118), kind=kLoop, calls=%fused_computation.9 | loop fusion | flops 1966080 | bytes 7864320 | tf_op jit(solution)/shard_map/sub | solution.py:110
  163.7 2.9 %copy.121 = f32[96,4096]{1,0:T(8,128)} copy(f32[96,4096]{0,1:T(8,128)} %get-tuple-element.20) | data formatting | bytes 3145728
  168.4 11.4 %reduce-scatter.7.cloned.1.call-done = f32[192,96]{1,0:T(8,128)} async-done(((f32[768,96]{1,0:T(8,128)}), f32[192,96]{1,0:T(8,128)}) %reduce-scatter.7.cloned.1.call-update) | async-done | bytes 73744
  (135 shorter events, 37.3 us)
Async XLA Ops:
  7.2 19.1 %copy-start = (s32[1,8,128]{2,1,0:T(8,128)S(1)}, s32[1,8,128]{2,1,0:T(8,128)}, u32[]{:S(2)}) copy-start(s32[1,8,128]{2,1,0:T(8,128)} %param.12) | copy-start | bytes 12292
  7.2 18.5 %copy-start.27 = (s32[1,8]{1,0:T(1,128)S(1)}, s32[1,8]{1,0:T(1,128)}, u32[]{:S(2)}) copy-start(s32[1,8]{1,0:T(1,128)} %param.13) | copy-start | bytes 100
  7.2 18.5 %copy-start.28 = (s32[1,8]{1,0:T(1,128)S(1)}, s32[1,8]{1,0:T(1,128)}, u32[]{:S(2)}) copy-start(s32[1,8]{1,0:T(1,128)} %param.14) | copy-start | bytes 100
  7.2 16.6 %collective-permute-start = (bf16[192,3072]{1,0:T(8,128)(2,1)}, bf16[192,3072]{1,0:T(8,128)(2,1)S(1)}, u32[]{:S(2)}, u32[]{:S(2)}) collective-permute-start(bf16[192,3072]{1,0:T(8,128)(2,1)} %param.17), channel_id=1, source_target_pairs={{0,8},{8,16},{16,24},{24,0},{1,9},{9,17},{17,25},{25,1},{2,10},{10... | collective-permute-start | bytes 3538952 | tf_op jit(solution)/shard_map/ppermute | solution.py:84
  23.8 15.7 %collective-permute-start.1 = (bf16[192,3072]{1,0:T(8,128)(2,1)S(1)}, bf16[192,3072]{1,0:T(8,128)(2,1)}, u32[]{:S(2)}, u32[]{:S(2)}) collective-permute-start(bf16[192,3072]{1,0:T(8,128)(2,1)S(1)} %collective-permute-done), channel_id=1, source_target_pairs={{0,8},{8,16},{16,24},{24,0},{1,9},{9,17},{17,25},{25,1},{2,10},{10... | collective-permute-start | bytes 3538952 | tf_op jit(solution)/shard_map/ppermute | solution.py:84
  39.5 21.5 %collective-permute-start.2 = (bf16[192,3072]{1,0:T(8,128)(2,1)}, bf16[192,3072]{1,0:T(8,128)(2,1)}, u32[]{:S(2)}, u32[]{:S(2)}) collective-permute-start(bf16[192,3072]{1,0:T(8,128)(2,1)} %collective-permute-done.1), channel_id=1, source_target_pairs={{0,8},{8,16},{16,24},{24,0},{1,9},{9,17},{17,25},{25,1},{2,10},{10... | collective-permute-start | bytes 3538952 | tf_op jit(solution)/shard_map/ppermute | solution.py:84
  41.2 15.3 %all-to-all-start = ((bf16[96,8,128]{2,0,1:T(8,128)(2,1)}), bf16[96,8,128]{2,0,1:T(8,128)(2,1)S(1)}, u32[]{:S(2)}, u32[]{:S(2)}) async-start(bf16[96,8,128]{2,0,1:T(8,128)(2,1)} %select_convert_fusion), calls=%async_computation | async-start | bytes 393216 | tf_op jit(solution)/shard_map/all_to_all | solution.py:76
  47.8 28.6 %all-gather.2.cloned.1.call-start = ((), (), s32[]{:S(2)}) async-start(), calls=%async_computation.4 | async-start | bytes 1474560 | tf_op jit(solution)/shard_map/all_gather | solution.py:92
  48.5 108.7 %reduce-scatter.5.cloned.1.call-start = ((), (), s32[]{:S(2)}) async-start(), calls=%async_computation.5 | async-start | bytes 2654208 | tf_op jit(solution)/shard_map/reduce_scatter | solution.py:114
  59.3 7.7 %copy-start.20 = (f32[128]{0:T(128)}, f32[128]{0:T(128)S(1)}, u32[]{:S(2)}) copy-start(f32[128]{0:T(128)S(1)} %broadcast_multiply_fusion.1) | copy-start | bytes 1540
  60.5 3.3 %copy-start.25 = (f32[128]{0:T(128)}, f32[128]{0:T(128)S(1)}, u32[]{:S(2)}) copy-start(f32[128]{0:T(128)S(1)} %fusion.26) | copy-start | bytes 1540
  61.0 6.0 %copy-start.23 = (f32[128]{0:T(128)}, f32[128]{0:T(128)S(1)}, u32[]{:S(2)}) copy-start(f32[128]{0:T(128)S(1)} %get-tuple-element.31) | copy-start | bytes 1540
  67.0 4.2 %copy-start.15 = (bf16[1536,3072]{1,0:T(8,128)(2,1)}, bf16[1536,3072]{1,0:T(8,128)(2,1)S(1)}, u32[]{:S(2)}) copy-start(bf16[1536,3072]{1,0:T(8,128)(2,1)S(1)} %constant_dynamic-update-slice_fusion) | copy-start | bytes 28311556
  76.4 3.8 %copy-start.6 = (bf16[128,3072]{1,0:T(8,128)(2,1)S(1)}, bf16[128,3072]{1,0:T(8,128)(2,1)}, u32[]{:S(2)}) copy-start(bf16[128,3072]{1,0:T(8,128)(2,1)} %copy-done.5) | copy-start | bytes 2359300
  86.9 6.4 %copy-start.9 = (bf16[12,128,128]{2,1,0:T(8,128)(2,1)S(1)}, bf16[12,128,128]{2,1,0:T(8,128)(2,1)}, u32[]{:S(2)}) copy-start(bf16[12,128,128]{2,1,0:T(8,128)(2,1)} %copy-done.8) | copy-start | bytes 1179652
  86.9 7.7 %copy-start.4 = (f32[768,128]{0,1:T(8,128)S(1)}, f32[768,128]{0,1:T(8,128)}, u32[]{:S(2)}) copy-start(f32[768,128]{0,1:T(8,128)} %copy.103) | copy-start | bytes 1179652
  86.9 7.7 %copy-start.21 = (f32[128]{0:T(128)S(1)}, f32[128]{0:T(128)}, u32[]{:S(2)}) copy-start(f32[128]{0:T(128)} %copy-done.20) | copy-start | bytes 1540
  86.9 7.7 %copy-start.29 = (f32[128]{0:T(128)S(1)}, f32[128]{0:T(128)}, u32[]{:S(2)}) copy-start(f32[128]{0:T(128)} %get-tuple-element.30) | copy-start | bytes 1540
  94.7 5.4 %copy-start.26 = (f32[128]{0:T(128)S(1)}, f32[128]{0:T(128)}, u32[]{:S(2)}) copy-start(f32[128]{0:T(128)} %copy-done.25) | copy-start | bytes 1540
  94.7 5.4 %copy-start.24 = (f32[128]{0:T(128)S(1)}, f32[128]{0:T(128)}, u32[]{:S(2)}) copy-start(f32[128]{0:T(128)} %copy-done.23) | copy-start | bytes 1540
  101.3 7.7 %copy-start.16 = (f32[192,96]{1,0:T(8,128)S(1)}, f32[192,96]{1,0:T(8,128)}, u32[]{:S(2)}) copy-start(f32[192,96]{1,0:T(8,128)} %param.19) | copy-start | bytes 221188
  101.4 21.2 %all-to-all-start.1 = ((f32[8,96,128]{2,1,0:T(8,128)}), f32[8,96,128]{2,1,0:T(8,128)S(1)}, u32[]{:S(2)}, u32[]{:S(2)}) async-start(f32[8,96,128]{2,1,0:T(8,128)} %bitcast.40), calls=%async_computation.1 | async-start | bytes 786432 | tf_op jit(solution)/shard_map/all_to_all | solution.py:105
  106.0 73.7 %reduce-scatter.7.cloned.1.call-start = ((), (), s32[]{:S(2)}) async-start(), calls=%async_computation.6 | async-start | bytes 491520
  163.7 2.9 %copy-start.1 = (f32[96,4096]{0,1:T(8,128)S(1)}, f32[96,4096]{0,1:T(8,128)}, u32[]{:S(2)}) copy-start(f32[96,4096]{0,1:T(8,128)} %get-tuple-element.21) | copy-start | bytes 4718596
  (14 other events, 20.0 us)
Sparse Core Ops, SparseCore 0:
  50.1 18.8 all-gather.1
  82.3 74.7 reduce-scatter.4
  159.7 20.0 reduce-scatter.6
